TPU v7x, 32 devices: a whole 2x2x4 slice. The times are simulated.
32 devices in a mesh: pts: 16 (over z, x, core), dom: 2 (over y).
Axes of the slice: x: 2, y: 2, z: 4, core: 2. Of those that a mesh axis runs over, the one named last changes fastest.
Arguments:
- vectors: bfloat16 [2, 4096, 768], P('dom', 'pts'), may hold values from -6 to 6
- neighbor_shards: int32 [2, 4096, 1], P('dom', 'pts'), may hold values from 0 to 15, as said below
- neighbor_locals: int32 [2, 4096, 32], P('dom', 'pts'), may hold values from 0 to 255
- partition: int32 [2, 4096], P('dom', 'pts'), may hold values from 0 to 1, as said below
Outputs:
- moved_vectors: bfloat16 [2, 4096, 768], P('dom', 'pts')
- moved_reverse: bfloat16 [2, 4096, 32], P('dom', 'pts')
- moved_join: bfloat16 [2, 4096, 32], P('dom', 'pts')
Inputs may be any that keep to these rules, and one draw needn't show every extreme that they name: `neighbor_shards`: the 1 numbers of one row are distinct, and the rows of one device come in aligned runs of 8 rows with equal numbers. Among the 256 rows of one device no number appears in more than 32 rows, and one number appears in exactly 32 rows. `partition`: for each id range, the 512 points of that range over all domains are split into 2 partitions of exactly 256 points each.
All inputs are finite; a program needn't handle non-finite values.
Results may differ from a plain program's by a relative error of at most 0.001.
Values may be sent and summed in bfloat16 or wider, within the bound.
A program may use at most 64 MiB of HBM per device.

v0:
```python
import jax
import jax.numpy as jnp
from jax import lax
from jax.sharding import PartitionSpec as P

D = 768
R = 32


BIG_VALUE = 1000000000.0


def merge_lowest(running, distance, allowed):
    masked = jnp.where(allowed, distance, BIG_VALUE)
    joined = jnp.concatenate([running, masked], axis=1)
    return -lax.top_k(-joined, running.shape[1])[0]


def finish_rows(lowest):
    return jnp.where(lowest < 0.5 * BIG_VALUE, lowest, 0.0)


def per_device(vectors, neighbor_shards, neighbor_locals, partition):
    pts_count = lax.axis_size("pts")
    dom_count = lax.axis_size("dom")
    position = lax.axis_index("pts")
    point_vec = vectors[0]
    nbr_shards = neighbor_shards[0]
    nbr_locals = neighbor_locals[0]
    assigned = partition[0]
    per_dev = point_vec.shape[0]
    width_w = nbr_shards.shape[1]
    list_len = nbr_locals.shape[1]
    row_cap = per_dev // 8
    slot_ids = jnp.arange(per_dev, dtype=jnp.int32)
    dom_ids = jnp.arange(dom_count, dtype=jnp.int32)
    part_count = jnp.sum((assigned[:, None] == dom_ids[None, :]).astype(jnp.int32), axis=0)
    part_order = jnp.argsort(assigned, stable=True)
    part_start = jnp.cumsum(part_count) - part_count
    source_pos = jnp.clip(part_start[:, None] + slot_ids[None, :], 0, per_dev - 1)
    part_source = part_order[source_pos]
    part_valid = slot_ids[None, :] < part_count[:, None]
    send_counts = part_count[:, None]

    def pack_part(values):
        return jnp.where(part_valid[:, :, None], values[part_source], jnp.zeros((), values.dtype))

    def unpack_part(received, piece_counts):
        flat_counts = piece_counts[:, 0]
        range_ends = jnp.cumsum(flat_counts)
        begins = range_ends - flat_counts
        sender = jnp.sum((range_ends[None, :] <= slot_ids[:, None]).astype(jnp.int32), axis=1)
        sender = jnp.minimum(sender, dom_count - 1)
        offset = slot_ids - begins[sender]
        flat_rows = received.reshape(dom_count * per_dev, received.shape[-1])
        return flat_rows[sender * per_dev + offset]

    targets = jnp.arange(pts_count, dtype=jnp.int32)
    member = jnp.sum((nbr_shards[:, :, None] == targets[None, None, :]).astype(jnp.int32), axis=1)
    send_order = jnp.argsort(1 - member.T, axis=1, stable=True)[:, :row_cap]
    send_count = jnp.sum(member, axis=0)
    send_valid = jnp.arange(row_cap, dtype=jnp.int32)[None, :] < send_count[:, None]
    send_vec = jnp.where(
        send_valid[:, :, None], point_vec[send_order], jnp.zeros((), point_vec.dtype)
    )
    send_ids = jnp.where(send_valid, position * per_dev + send_order, -1)
    own_global = position * per_dev + slot_ids
    slot_shard = nbr_shards[:, jnp.arange(list_len) % width_w]
    send_info = (slot_shard * per_dev + nbr_locals)[send_order]
    send_info = jnp.where(send_valid[:, :, None], send_info, -1)
    recv_vec, recv_ids, recv_info = (
        lax.all_to_all(send_vec, "pts", split_axis=0, concat_axis=0, tiled=True),
        lax.all_to_all(send_ids, "pts", split_axis=0, concat_axis=0, tiled=True),
        lax.all_to_all(send_info, "pts", split_axis=0, concat_axis=0, tiled=True),
    )
    total_rows = pts_count * row_cap
    block_rows = 512
    blocks = total_rows // block_rows
    info_len = recv_info.shape[-1]
    block_vec = recv_vec.reshape(blocks, block_rows, point_vec.shape[1])
    block_ids = recv_ids.reshape(blocks, block_rows)
    block_info = recv_info.reshape(blocks, block_rows, info_len)
    own_norm = jnp.sum(jnp.square(point_vec.astype(jnp.float32)), axis=1)

    def join_block(running, pieces):
        reverse_top, join_top = running
        piece_vec, piece_ids, piece_info = pieces
        inner_prod = lax.dot_general(
            point_vec, piece_vec, (((1,), (1,)), ((), ())), preferred_element_type=jnp.float32
        )
        piece_norm = jnp.sum(jnp.square(piece_vec.astype(jnp.float32)), axis=1)
        distance = (own_norm[:, None] + piece_norm[None, :] - 2.0 * inner_prod) / D
        join_ok = (piece_ids[None, :] >= 0) & (piece_ids[None, :] != own_global[:, None])
        listed = jnp.any(piece_info[None, :, :] == own_global[:, None, None], axis=2)
        return (
            (
                merge_lowest(reverse_top, distance, join_ok & listed),
                merge_lowest(join_top, distance, join_ok),
            ),
            None,
        )

    start_rows = jnp.full((per_dev, R), BIG_VALUE, jnp.float32)
    (reverse_top, join_top), unused = lax.scan(
        join_block, (start_rows, start_rows), (block_vec, block_ids, block_info)
    )
    rows_pair = jnp.concatenate([finish_rows(reverse_top), finish_rows(join_top)], axis=1).astype(
        jnp.bfloat16
    )
    moved_vec, moved_rows, moved_counts = (
        lax.all_to_all(pack_part(point_vec), "dom", split_axis=0, concat_axis=0, tiled=True),
        lax.all_to_all(pack_part(rows_pair), "dom", split_axis=0, concat_axis=0, tiled=True),
        lax.all_to_all(send_counts, "dom", split_axis=0, concat_axis=0, tiled=True),
    )
    out_vec = unpack_part(moved_vec, moved_counts)
    out_rows = unpack_part(moved_rows, moved_counts)
    return (out_vec[None], out_rows[None, :, :R], out_rows[None, :, R:])


def solution(mesh):
    return jax.shard_map(
        per_device,
        mesh=mesh,
        in_specs=(
            P("dom", "pts", None),
            P("dom", "pts", None),
            P("dom", "pts", None),
            P("dom", "pts"),
        ),
        out_specs=(P("dom", "pts", None), P("dom", "pts", None), P("dom", "pts", None)),
        check_vma=False,
    )
```

profile of v0, /device:TPU:0, one launch (start us, length us, event | category | flops | bytes accessed | tf_op | source)
XLA Modules:
  0.0 177.6 jit_solution(13158831862825408658)
XLA Ops:
  7.2 0.8 fusion.6
  8.0 0.7 copy.31
  8.6 4.3 %all-to-all-start.1 = ((s32[2,1,1]{2,1,0:T(1,128)}), s32[2,1,1]{2,1,0:T(1,128)S(1)}, u32[]{:S(2)}, u32[]{:S(2)}) async-start(s32[2,1,1]{2,1,0:T(1,128)} %copy.31), calls=%async_computation.1 | async-start | bytes 2048 | tf_op jit(solution)/shard_map/all_to_all | solution.py:113
  12.9 1.3 convert_subtract_fusion
  14.2 0.6 iota.62
  14.8 0.8 convert_reduce_fusion
  15.6 0.7 broadcast_multiply_fusion
  16.4 0.9 copy.32
  17.3 0.2 reduce-window.16
  17.6 3.9 %sort.40 = (s32[256]{0:T(256)}, s32[256]{0:T(256)S(1)}) sort(s32[256]{0:T(256)} %bitcast.69, s32[256]{0:T(256)S(1)} %iota.60), dimensions={0}, to_apply=%region_1.0 | sort | flops 2048 | bytes 4096 | tf_op jit(solution)/shard_map/jit(argsort)/sort | solution.py:38
  21.4 3.5 %gather_fusion = s32[512]{0:T(512)S(1)} fusion(s32[256]{0:T(256)S(1)} %get-tuple-element.36, s32[1024]{0:T(1024)S(1)} %pad_clamp_fusion.3), kind=kCustom, calls=%fused_computation | custom fusion | bytes 6144 | tf_op jit(solution)/shard_map/gather | solution.py:41
  25.1 2.0 %gather_fusion.1 = bf16[512,768]{1,0:T(8,128)(2,1)S(1)} fusion(bf16[256,768]{1,0:T(8,128)(2,1)S(1)} %bitcast.50, s32[1024]{0:T(1024)S(1)} %pad_clamp_fusion.2), kind=kCustom, calls=%fused_computation.1 | custom fusion | bytes 1574912 | tf_op jit(solution)/shard_map/gather | solution.py:46
  27.1 1.0 broadcast_select_fusion.1
  28.4 1.4 add_select_fusion
  29.8 1.0 gather_fusion.3
  30.9 6.3 %all-to-all-start.2 = ((s32[16,1,32]{2,1,0:T(1,128)}), s32[16,1,32]{2,1,0:T(1,128)S(1)}, u32[]{:S(2)}, u32[]{:S(2)}) async-start(s32[16,1,32]{2,1,0:T(1,128)} %bitcast.14), calls=%async_computation.2 | async-start | bytes 16384 | tf_op jit(solution)/shard_map/all_to_all | solution.py:73
  37.3 2.0 %gather_fusion.4 = bf16[512,768]{1,0:T(8,128)(2,1)S(1)} fusion(bf16[256,768]{1,0:T(8,128)(2,1)S(1)} %bitcast.51, s32[1024]{0:T(1024)S(1)} %pad_clamp_fusion), kind=kCustom, calls=%fused_computation.4 | custom fusion | bytes 1574912 | tf_op jit(solution)/shard_map/gather | solution.py:64
  39.4 0.8 reshape.360
  40.1 3.4 %all-to-all-done.2 = s32[16,1,32]{2,1,0:T(1,128)S(1)} async-done(((s32[16,1,32]{2,1,0:T(1,128)}), s32[16,1,32]{2,1,0:T(1,128)S(1)}, u32[]{:S(2)}, u32[]{:S(2)}) %all-to-all-start.2) | async-done | bytes 2080 | tf_op jit(solution)/shard_map/all_to_all | solution.py:73
  43.5 3.5 %all-to-all-start.3 = ((s32[16,1,1024]{2,1,0:T(1,128)}), s32[16,1,1024]{2,1,0:T(1,128)S(1)}, u32[]{:S(2)}, u32[]{:S(2)}) async-start(s32[16,1,1024]{2,1,0:T(1,128)} %reshape.360), calls=%async_computation.3 | async-start | bytes 131072 | tf_op jit(solution)/shard_map/all_to_all | solution.py:74
  47.0 1.0 broadcast_select_fusion
  48.1 5.8 %all-to-all-done.3 = s32[16,1,1024]{2,1,0:T(1,128)S(1)} async-done(((s32[16,1,1024]{2,1,0:T(1,128)}), s32[16,1,1024]{2,1,0:T(1,128)S(1)}, u32[]{:S(2)}, u32[]{:S(2)}) %all-to-all-start.3) | async-done | bytes 65568 | tf_op jit(solution)/shard_map/all_to_all | solution.py:74
  53.9 3.6 %all-to-all-start.4 = ((bf16[16,32,768]{2,1,0:T(8,128)(2,1)}), bf16[16,32,768]{2,1,0:T(8,128)(2,1)S(1)}, u32[]{:S(2)}, u32[]{:S(2)}) async-start(bf16[16,32,768]{2,1,0:T(8,128)(2,1)} %broadcast_select_fusion), calls=%async_computation.4 | async-start | bytes 1572864 | tf_op jit(solution)/shard_map/all_to_all | solution.py:72
  57.7 0.2 reduce-window.17
  57.8 0.6 fusion.13
  58.5 1.3 compare_select_fusion.5
  59.8 0.5 broadcast.319
  60.4 0.7 reduce.6
  61.1 0.5 broadcast.320
  61.6 0.8 reduce.7
  62.7 1.8 %compare_reduce_fusion = pred[256,512]{1,0:T(8,128)(4,1)S(1)} fusion(s32[512,32]{0,1:T(8,128)S(1)} %copy.33, s32[256]{0:T(256)S(1)} %iota_add_fusion), kind=kLoop, calls=%fused_computation.7 | loop fusion | flops 8257536 | bytes 197632 | tf_op jit(solution)/shard_map/while/body/eval_jaxpr/reduce_or | solution.py:94
  64.5 0.2 copy.34
  64.7 11.5 %all-to-all-done.4 = bf16[16,32,768]{2,1,0:T(8,128)(2,1)S(1)} async-done(((bf16[16,32,768]{2,1,0:T(8,128)(2,1)}), bf16[16,32,768]{2,1,0:T(8,128)(2,1)S(1)}, u32[]{:S(2)}, u32[]{:S(2)}) %all-to-all-start.4) | async-done | bytes 786464 | tf_op jit(solution)/shard_map/all_to_all | solution.py:72
  76.2 3.5 %all-to-all-start = ((bf16[2,256,768]{2,1,0:T(8,128)(2,1)}), bf16[2,256,768]{2,1,0:T(8,128)(2,1)S(1)}, u32[]{:S(2)}, u32[]{:S(2)}) async-start(bf16[2,256,768]{2,1,0:T(8,128)(2,1)} %broadcast_select_fusion.1), calls=%async_computation | async-start | bytes 1572864 | tf_op jit(solution)/shard_map/all_to_all | solution.py:111
  79.7 0.2 multiply_reduce_fusion
  80.0 0.5 and_select_fusion
  80.7 38.9 %top_k.14 = (f32[256,544]{0,1:T(8,128)S(1)}, s32[256,544]{0,1:T(8,128)}) sort(f32[256,544]{0,1:T(8,128)S(1)} %get-tuple-element.68, s32[256,544]{0,1:T(8,128)S(1)} %iota.64.clone), dimensions={1}, to_apply=%region_10.11 | sort | flops 2506752 | bytes 2228224 | tf_op jit(solution)/shard_map/while/body/eval_jaxpr/top_k | solution.py:16
  119.5 0.2 copy.43
  119.8 38.7 %top_k.20 = (f32[256,544]{0,1:T(8,128)S(1)}, s32[256,544]{0,1:T(8,128)}) sort(f32[256,544]{0,1:T(8,128)S(1)} %get-tuple-element.67, s32[256,544]{0,1:T(8,128)S(1)} %iota.64.clone), dimensions={1}, to_apply=%region_11.12 | sort | flops 2506752 | bytes 2228224 | tf_op jit(solution)/shard_map/while/body/eval_jaxpr/top_k | solution.py:16
  158.5 0.2 copy.47
  158.9 1.3 gather_fusion.5
  160.3 0.6 broadcast_select_fusion.3
  160.9 3.3 %all-to-all-start.5 = ((bf16[2,256,64]{1,2,0:T(8,128)(2,1)}), bf16[2,256,64]{1,2,0:T(8,128)(2,1)S(1)}, u32[]{:S(2)}, u32[]{:S(2)}) async-start(bf16[2,256,64]{1,2,0:T(8,128)(2,1)} %broadcast_select_fusion.3), calls=%async_computation.5 | async-start | bytes 131072 | tf_op jit(solution)/shard_map/all_to_all | solution.py:112
  164.3 1.9 %gather_fusion.2 = bf16[256,768]{1,0:T(8,128)(2,1)} fusion(bf16[512,768]{1,0:T(8,128)(2,1)S(1)} %bitcast.52, s32[1024]{0:T(1024)S(1)} %pad_clamp_fusion.1), kind=kCustom, calls=%fused_computation.2 | custom fusion | bytes 787456 | tf_op jit(solution)/shard_map/gather | solution.py:56
  166.2 2.2 %all-to-all-done.5 = bf16[2,256,64]{1,2,0:T(8,128)(2,1)S(1)} async-done(((bf16[2,256,64]{1,2,0:T(8,128)(2,1)}), bf16[2,256,64]{1,2,0:T(8,128)(2,1)S(1)}, u32[]{:S(2)}, u32[]{:S(2)}) %all-to-all-start.5) | async-done | bytes 65568 | tf_op jit(solution)/shard_map/all_to_all | solution.py:112
  168.5 0.9 gather_fusion.6
  169.4 0.7 copy.39
  170.1 0.7 copy.40
  (42 shorter events, 2.0 us)
Async XLA Ops:
  8.6 22.2 %all-to-all-start.1 = ((s32[2,1,1]{2,1,0:T(1,128)}), s32[2,1,1]{2,1,0:T(1,128)S(1)}, u32[]{:S(2)}, u32[]{:S(2)}) async-start(s32[2,1,1]{2,1,0:T(1,128)} %copy.31), calls=%async_computation.1 | async-start | bytes 2048 | tf_op jit(solution)/shard_map/all_to_all | solution.py:113
  12.9 15.5 %sort.43.cloned.1.call-start = ((), (), s32[]{:S(2)}) async-start(), calls=%async_computation.6 | async-start | bytes 98336 | tf_op jit(solution)/shard_map/jit(argsort)/sort | solution.py:60
  21.4 3.7 %copy-start = (bf16[1,256,768]{2,1,0:T(8,128)(2,1)S(1)}, bf16[1,256,768]{2,1,0:T(8,128)(2,1)}, u32[]{:S(2)}) copy-start(bf16[1,256,768]{2,1,0:T(8,128)(2,1)} %param.4) | copy-start | bytes 1179652
  30.9 12.7 %all-to-all-start.2 = ((s32[16,1,32]{2,1,0:T(1,128)}), s32[16,1,32]{2,1,0:T(1,128)S(1)}, u32[]{:S(2)}, u32[]{:S(2)}) async-start(s32[16,1,32]{2,1,0:T(1,128)} %bitcast.14), calls=%async_computation.2 | async-start | bytes 16384 | tf_op jit(solution)/shard_map/all_to_all | solution.py:73
  43.5 10.4 %all-to-all-start.3 = ((s32[16,1,1024]{2,1,0:T(1,128)}), s32[16,1,1024]{2,1,0:T(1,128)S(1)}, u32[]{:S(2)}, u32[]{:S(2)}) async-start(s32[16,1,1024]{2,1,0:T(1,128)} %reshape.360), calls=%async_computation.3 | async-start | bytes 131072 | tf_op jit(solution)/shard_map/all_to_all | solution.py:74
  53.9 22.3 %all-to-all-start.4 = ((bf16[16,32,768]{2,1,0:T(8,128)(2,1)}), bf16[16,32,768]{2,1,0:T(8,128)(2,1)S(1)}, u32[]{:S(2)}, u32[]{:S(2)}) async-start(bf16[16,32,768]{2,1,0:T(8,128)(2,1)} %broadcast_select_fusion), calls=%async_computation.4 | async-start | bytes 1572864 | tf_op jit(solution)/shard_map/all_to_all | solution.py:72
  76.2 84.8 %all-to-all-start = ((bf16[2,256,768]{2,1,0:T(8,128)(2,1)}), bf16[2,256,768]{2,1,0:T(8,128)(2,1)S(1)}, u32[]{:S(2)}, u32[]{:S(2)}) async-start(bf16[2,256,768]{2,1,0:T(8,128)(2,1)} %broadcast_select_fusion.1), calls=%async_computation | async-start | bytes 1572864 | tf_op jit(solution)/shard_map/all_to_all | solution.py:111
  160.9 7.4 %all-to-all-start.5 = ((bf16[2,256,64]{1,2,0:T(8,128)(2,1)}), bf16[2,256,64]{1,2,0:T(8,128)(2,1)S(1)}, u32[]{:S(2)}, u32[]{:S(2)}) async-start(bf16[2,256,64]{1,2,0:T(8,128)(2,1)} %broadcast_select_fusion.3), calls=%async_computation.5 | async-start | bytes 131072 | tf_op jit(solution)/shard_map/all_to_all | solution.py:112
Sparse Core Ops, SparseCore 0:
  16.6 2.2 sort.45.cloned.1.call-done
  (1 shorter events, 0.0 us)
where the time goes:
time: 179 us; the launch traced here: 178 us
  other arithmetic  95.3 us (53%)
  starting transfers between devices  24.5 us (14%)
  waiting for transfers between devices  22.9 us (13%)
  local copies, waits for them, and re-layouts  20.2 us (11%)
  between operations  14.3 us (8%)
    top_k x2, other arithmetic, merge_lowest(): return -lax.top_k(-joined, running.shape[1])[0]  77.5 us
    all_to_all x1, waiting for transfers between devices, per_device(): lax.all_to_all(send_vec, 'pts', split_axis=0, concat_axis=0, tiled=True)  11.5 us
    all_to_all x1, starting transfers between devices, per_device(): lax.all_to_all(send_ids, 'pts', split_axis=0, concat_axis=0, tiled=True)  6.31 us
    all_to_all x1, waiting for transfers between devices, per_device(): lax.all_to_all(send_info, 'pts', split_axis=0, concat_axis=0, tiled=True)  5.81 us
    all_to_all x1, starting transfers between devices, per_device(): lax.all_to_all(send_counts, 'dom', split_axis=0, concat_axis=0, tiled=True)  4.26 us
    sort x1, other arithmetic, per_device(): part_order = jnp.argsort(assigned, stable=True)  3.87 us
    all_to_all x1, starting transfers between devices, per_device(): lax.all_to_all(send_vec, 'pts', split_axis=0, concat_axis=0, tiled=True)  3.61 us
  transfers between devices with their start and end apart: 6, of which 4 were waited for; matrix products, arithmetic and copies ran while one was open for 63% of the time, Pallas kernels for 0%

commit v1 on v0

v1 whole, which is shorter than its diff:
```python
import functools

import jax
import jax.numpy as jnp
from jax import lax
from jax.experimental import pallas as pl
from jax.experimental.pallas import tpu as pltpu
from jax.sharding import PartitionSpec as P

R = 32
BIG = 1.0e9
NT = (((1,), (1,)), ((), ()))
SHIFT = 1024


def oddeven_pairs(count):
    pairs = []

    def merge(lo, hi, r):
        step = r * 2
        if step < hi - lo:
            merge(lo, hi, step)
            merge(lo + r, hi, step)
            pairs.extend((i, i + r) for i in range(lo + r, hi - r, step))
        else:
            pairs.append((lo, lo + r))

    def sort(lo, hi):
        if hi - lo >= 1:
            mid = lo + (hi - lo) // 2
            sort(lo, mid)
            sort(mid + 1, hi)
            merge(lo, hi, 1)

    sort(0, count - 1)
    return pairs


PAIRS = oddeven_pairs(R)


def exchange(items, i, j):
    a, b = items[i], items[j]
    items[i], items[j] = jnp.minimum(a, b), jnp.maximum(a, b)


def sort_list(items):
    items = list(items)
    for i, j in PAIRS:
        exchange(items, i, j)
    return items


def merge_low(first, second):
    items = [jnp.minimum(first[i], second[R - 1 - i]) for i in range(R)]
    half = R // 2
    while half:
        for i in range(R):
            if not i & half:
                exchange(items, i, i + half)
        half //= 2
    return items


def dot(a, b):
    return jnp.dot(a, b, preferred_element_type=jnp.float32)


def dot_nt(a, b):
    return lax.dot_general(a, b, NT, preferred_element_type=jnp.float32)


def iota(shape, dim):
    return lax.broadcasted_iota(jnp.int32, shape, dim)


def onehot(cond):
    return jnp.where(cond, 1.0, 0.0).astype(jnp.bfloat16)


def kernel(n, doms, cap, *refs):
    refs = list(refs)
    vec, shards_t, locs, part = refs[:4]
    refs = refs[4:]
    wide = shards_t.shape[0] > 1
    slot_shard = refs.pop(0) if wide else None
    out_vec, out_rev, out_join = refs[:3]
    (sbuf, sinfo, rvec, rinfo, dvec, dpart, posn, ltile, lshard, onorm, dist, lists, rows, srows, drows,
     vs_sem, vr_sem, is_sem, ir_sem, ds_sem, dr_sem, ps_sem, pr_sem, rs_sem, rr_sem) = refs[3:]
    per, depth = vec.shape
    list_len = locs.shape[1]
    groups = cap // 8
    lanes = groups * list_len
    me = lax.axis_index("pts")
    dom = lax.axis_index("dom")
    bar = pltpu.get_barrier_semaphore()

    def greet_pts(o, carry):
        pl.semaphore_signal(bar, inc=1, device_id={"pts": lax.rem(me + o, n)}, device_id_type=pl.DeviceIdType.MESH)
        return carry

    def greet_dom(o, carry):
        pl.semaphore_signal(bar, inc=1, device_id={"dom": lax.rem(dom + o, doms)}, device_id_type=pl.DeviceIdType.MESH)
        return carry

    lax.fori_loop(1, n, greet_pts, 0)
    lax.fori_loop(1, doms, greet_dom, 0)

    own = vec[...]
    upper = onehot(iota((per, per), 0) < iota((per, per), 1))
    targets = iota((n, per), 0)
    member = shards_t[0:1, :] == targets
    for w in range(1, shards_t.shape[0]):
        member = member | (shards_t[w : w + 1, :] == targets)
    rank = dot(onehot(member), upper)
    posn[...] = jnp.where(member, rank, -1.0)
    tile = onehot(lax.rem(iota((list_len, lanes), 1), list_len) == iota((list_len, lanes), 0))
    ltile[...] = (dot(locs[...].astype(jnp.float32).astype(jnp.bfloat16), tile) + 1.0).astype(jnp.bfloat16)
    if wide:
        lshard[...] = dot(slot_shard[...].astype(jnp.float32).astype(jnp.bfloat16), tile)
    id_tile = (iota((per, lanes), 0) + 1).astype(jnp.float32).astype(jnp.bfloat16)
    lane_group = iota((8, lanes), 1) // list_len

    def pack(c, carry):
        row = posn[pl.ds(c, 1), :]
        pick = onehot(row == iota((cap, per), 0).astype(jnp.float32))
        sbuf[c] = dot(pick, own).astype(jnp.bfloat16)
        entry = ltile[...]
        if wide:
            entry = jnp.where(lshard[...] == c.astype(jnp.float32), entry.astype(jnp.float32), 0.0).astype(jnp.bfloat16)
        full = dot(pick, entry) + SHIFT * dot(pick, id_tile)
        flat = jnp.zeros((8, lanes), jnp.float32)
        for g in range(groups):
            flat = jnp.where(lane_group == g, full[8 * g : 8 * g + 8], flat)
        sinfo[c] = flat.astype(jnp.int32)
        return carry

    lax.fori_loop(0, n, pack, 0)
    square = jnp.square(own.astype(jnp.float32))
    high = square.astype(jnp.bfloat16)
    low = (square - high.astype(jnp.float32)).astype(jnp.bfloat16)
    ones = jnp.ones((8, depth), jnp.bfloat16)
    onorm[...] = dot_nt(ones, high) + dot_nt(ones, low)

    pl.semaphore_wait(bar, n - 1 + doms - 1)

    def vec_copy(c, slot_s, slot_r):
        return pltpu.make_async_remote_copy(
            src_ref=sbuf.at[c], dst_ref=rvec.at[slot_r], send_sem=vs_sem.at[slot_s], recv_sem=vr_sem.at[slot_r],
            device_id={"pts": c}, device_id_type=pl.DeviceIdType.MESH)

    def info_copy(c, slot_s, slot_r):
        return pltpu.make_async_remote_copy(
            src_ref=sinfo.at[c], dst_ref=rinfo.at[slot_r], send_sem=is_sem.at[slot_s], recv_sem=ir_sem.at[slot_r],
            device_id={"pts": c}, device_id_type=pl.DeviceIdType.MESH)

    def dom_copy(c, slot_r, src, dst, send, recv):
        return pltpu.make_async_remote_copy(
            src_ref=src, dst_ref=dst.at[slot_r], send_sem=send.at[c], recv_sem=recv.at[slot_r],
            device_id={"dom": c}, device_id_type=pl.DeviceIdType.MESH)

    def send_dom(o, carry):
        c = lax.rem(dom + o, doms)
        dom_copy(c, dom, part, dpart, ps_sem, pr_sem).start()
        dom_copy(c, dom, vec, dvec, ds_sem, dr_sem).start()
        return carry

    def send_pts(o, carry):
        c = lax.rem(me + o, n)
        info_copy(c, c, me).start()
        vec_copy(c, c, me).start()
        return carry

    lax.fori_loop(1, doms, send_dom, 0)
    lax.fori_loop(1, n, send_pts, 0)

    rvec[me] = sbuf[me]
    rinfo[me] = sinfo[me]
    dvec[dom] = own
    dpart[dom] = part[...]
    point = iota((8, per), 1) + 1

    def join(s, same):
        cand = rvec[s]
        wide_cand = cand.astype(jnp.float32)
        norm = jnp.sum(wide_cand * wide_cand, axis=1, keepdims=True)
        value = (onorm[0:1, :] + norm - 2.0 * dot_nt(cand, vec[...])) * (1.0 / depth)
        info = rinfo[s]
        ids = lax.div(info, SHIFT)
        entry = info - ids * SHIFT
        reverse, joined = [], []
        for g in range(groups):
            at = g * list_len
            listed = entry[:, at : at + 1] == point
            for k in range(1, list_len):
                listed = listed | (entry[:, at + k : at + k + 1] == point)
            slot_id = ids[:, at : at + 1]
            allowed = slot_id > 0
            if same:
                allowed = allowed & (slot_id != point)
            block = jnp.where(allowed, value[8 * g : 8 * g + 8], BIG)
            joined.append(block)
            reverse.append(jnp.where(listed, block, BIG))
        dist[0, s] = jnp.concatenate(reverse, axis=0).astype(jnp.bfloat16)
        dist[1, s] = jnp.concatenate(joined, axis=0).astype(jnp.bfloat16)

    join(me, True)

    def take(o, carry):
        s = lax.rem(me + n - o, n)
        info_copy(s, s, s).wait_recv()
        vec_copy(s, s, s).wait_recv()
        join(s, False)
        return carry

    def take_dom(o, carry):
        s = lax.rem(dom + doms - o, doms)
        dom_copy(s, s, part, dpart, ps_sem, pr_sem).wait_recv()
        dom_copy(s, s, vec, dvec, ds_sem, dr_sem).wait_recv()
        return carry

    def selections():
        base = jnp.zeros((8, 1), jnp.float32)
        for d in range(doms):
            here = jnp.broadcast_to(dpart[d], (8, per)) == dom
            flag = jnp.where(here, 1.0, 0.0)
            place = jnp.where(here, dot(flag.astype(jnp.bfloat16), upper) + base, -1.0)
            base = base + jnp.sum(flag, axis=1, keepdims=True)
            yield d, onehot(place[0:1, :] == iota((per, per), 0).astype(jnp.float32))

    half = n // 2
    lax.fori_loop(1, half, take, 0)
    lax.fori_loop(1, doms, take_dom, 0)
    total = jnp.zeros((per, depth), jnp.float32)
    for d, pick in selections():
        total = total + dot(pick, dvec[d])
    out_vec[...] = total.astype(jnp.bfloat16)
    lax.fori_loop(half, n, take, 0)

    blocks = cap // 16
    sources = R // blocks
    chunks = n // sources
    tiles = per // 128

    def sort_one(which, tile_id):
        columns = slice(tile_id * 128, tile_id * 128 + 128)

        def chunk(t):
            items = []
            for a in range(sources):
                for b in range(blocks):
                    items.append(dist[which, t * sources + a, 16 * b : 16 * b + 16, columns])
            items = [x.astype(jnp.float32) for x in sort_list(items)]
            return merge_low([x[:8] for x in items], [x[8:] for x in items])

        if chunks == 1:
            items = chunk(0)
            for i in range(R):
                lists[tile_id, i] = items[i]
        else:
            for i in range(R):
                lists[tile_id, i] = jnp.full((8, 128), BIG, jnp.float32)

            def more(t, carry):
                items = merge_low([lists[tile_id, i] for i in range(R)], chunk(t))
                for i in range(R):
                    lists[tile_id, i] = items[i]
                return carry

            lax.fori_loop(0, chunks, more, 0)

    upper_half = iota((8, 128), 0) < 4

    def both(which, carry):
        for tile_id in range(tiles):
            sort_one(which, tile_id)
        for pair in range(tiles // 2):
            first, second = [], []
            for i in range(R):
                a, b = lists[2 * pair, i], lists[2 * pair + 1, i]
                first.append(jnp.where(upper_half, a, b))
                second.append(pltpu.roll(jnp.where(upper_half, b, a), 4, 0))
            items = merge_low(first, second)
            for shift in (6, 7):
                items = merge_low(items, [pltpu.roll(x, shift, 0) for x in items])
            for i in range(R):
                x = jnp.where(items[i] < 0.5 * BIG, items[i], 0.0)
                rows[which, i : i + 1, 256 * pair : 256 * pair + 128] = x[0:1]
                rows[which, i : i + 1, 256 * pair + 128 : 256 * pair + 256] = x[4:5]
        srows[which] = rows[which].astype(jnp.bfloat16)
        return carry

    lax.fori_loop(0, 2, both, 0)

    def send_rows(o, carry):
        dom_copy(lax.rem(dom + o, doms), dom, srows, drows, rs_sem, rr_sem).start()
        return carry

    lax.fori_loop(1, doms, send_rows, 0)
    drows[dom] = srows[...]

    def take_rows(o, carry):
        s = lax.rem(dom + doms - o, doms)
        dom_copy(s, s, srows, drows, rs_sem, rr_sem).wait_recv()
        return carry

    lax.fori_loop(1, doms, take_rows, 0)
    total_rev = jnp.zeros((per, R), jnp.float32)
    total_join = jnp.zeros((per, R), jnp.float32)
    for d, pick in selections():
        total_rev = total_rev + dot_nt(pick, drows[d, 0])
        total_join = total_join + dot_nt(pick, drows[d, 1])
    out_rev[...] = total_rev.astype(jnp.bfloat16)
    out_join[...] = total_join.astype(jnp.bfloat16)

    def drain_pts(o, carry):
        c = lax.rem(me + o, n)
        info_copy(c, c, me).wait_send()
        vec_copy(c, c, me).wait_send()
        return carry

    def drain_dom(o, carry):
        c = lax.rem(dom + o, doms)
        dom_copy(c, dom, part, dpart, ps_sem, pr_sem).wait_send()
        dom_copy(c, dom, vec, dvec, ds_sem, dr_sem).wait_send()
        dom_copy(c, dom, srows, drows, rs_sem, rr_sem).wait_send()
        return carry

    lax.fori_loop(1, n, drain_pts, 0)
    lax.fori_loop(1, doms, drain_dom, 0)


def solution(mesh):
    n, doms = mesh.shape["pts"], mesh.shape["dom"]

    def per_device(vectors, neighbor_shards, neighbor_locals, partition):
        per, depth = vectors.shape[1:]
        width = neighbor_shards.shape[2]
        list_len = neighbor_locals.shape[2]
        cap = per // 8
        lanes = (cap // 8) * list_len
        operands = [vectors[0], neighbor_shards[0].T, neighbor_locals[0], partition]
        if width > 1:
            operands.append(neighbor_shards[0][:, jnp.arange(list_len) % width])
        bf16, f32, i32 = jnp.bfloat16, jnp.float32, jnp.int32
        dma = pltpu.SemaphoreType.DMA
        vmem = pl.BlockSpec(memory_space=pltpu.VMEM)
        out_vec, out_rev, out_join = pl.pallas_call(
            functools.partial(kernel, n, doms, cap),
            out_shape=(
                jax.ShapeDtypeStruct((per, depth), bf16),
                jax.ShapeDtypeStruct((per, R), bf16),
                jax.ShapeDtypeStruct((per, R), bf16),
            ),
            in_specs=[vmem] * len(operands),
            out_specs=(vmem, vmem, vmem),
            scratch_shapes=[
                pltpu.VMEM((n, cap, depth), bf16),
                pltpu.VMEM((n, 8, lanes), i32),
                pltpu.VMEM((n, cap, depth), bf16),
                pltpu.VMEM((n, 8, lanes), i32),
                pltpu.VMEM((doms, per, depth), bf16),
                pltpu.VMEM((doms, 1, per), i32),
                pltpu.VMEM((n, per), f32),
                pltpu.VMEM((per, lanes), bf16),
                pltpu.VMEM((per, lanes), f32),
                pltpu.VMEM((8, per), f32),
                pltpu.VMEM((2, n, cap, per), bf16),
                pltpu.VMEM((per // 128, R, 8, 128), f32),
                pltpu.VMEM((2, R, per), f32),
                pltpu.VMEM((2, R, per), bf16),
                pltpu.VMEM((doms, 2, R, per), bf16),
                dma((n,)), dma((n,)), dma((n,)), dma((n,)),
                dma((doms,)), dma((doms,)), dma((doms,)), dma((doms,)), dma((doms,)), dma((doms,)),
            ],
            compiler_params=pltpu.CompilerParams(collective_id=0, has_side_effects=True),
        )(*operands)
        return out_vec[None], out_rev[None], out_join[None]

    return jax.shard_map(
        per_device,
        mesh=mesh,
        in_specs=(
            P("dom", "pts", None),
            P("dom", "pts", None),
            P("dom", "pts", None),
            P("dom", "pts"),
        ),
        out_specs=(P("dom", "pts", None), P("dom", "pts", None), P("dom", "pts", None)),
        check_vma=False,
    )
```

time: 179 us -> 39.9 us (0.22)
  the two profiles are of different devices: /device:TPU:0 before, /device:TPU:25 now
where the time goes in v1:
time: 39.9 us; the launch traced here: 39.6 us
  Pallas kernels  33.4 us (84%)
  local copies, waits for them, and re-layouts  5.53 us (14%)
  between operations  0.65 us (2%)
    pallas_call x1, Pallas kernels, per_device(): pl.pallas_call(functools.partial(kernel, n, doms, cap), out_shape=(jax.Sh...  33.4 us
    unnamed x6, local copies, waits for them, and re-layouts  5.53 us

profile of v1, /device:TPU:25, one launch (start us, length us, event | category | flops | bytes accessed | tf_op | source)
XLA Modules:
  0.0 39.6 jit_solution(10606187400091972829)
XLA Ops:
  0.6 1.5 %copy.7 = s32[1,256,32]{2,1,0:T(8,128)} copy(s32[1,256,32]{1,2,0:T(8,128)} %param.6) | data formatting | bytes 65536 | tf_op args[2]
  2.1 33.4 %shard_map.67 = (bf16[256,768]{1,0:T(8,128)(2,1)}, bf16[256,32]{1,0:T(8,128)(2,1)}, bf16[256,32]{1,0:T(8,128)(2,1)}) custom-call(bf16[256,768]{1,0:T(8,128)(2,1)} %bitcast.8, s32[1,256]{1,0:T(1,128)} %bitcast.11, s32[256,32]{1,0:T(8,128)} %bitcast.6, s32[1,256]{1,0:T(1,128)} %refs_3_.1), custom_call_target="tpu_custom_call" | custom-call | tf_op jit(solution)/shard_map/pallas_call | solution.py:348
  35.6 0.0 copy-start
  35.6 1.6 %copy.8 = bf16[1,256,32]{1,2,0:T(8,128)(2,1)} copy(bf16[1,256,32]{2,1,0:T(8,128)(2,1)} %bitcast.10) | data formatting | bytes 32768
  37.2 0.0 copy-done
  37.2 0.7 %copy.9 = bf16[1,256,32]{1,2,0:T(8,128)(2,1)} copy(bf16[1,256,32]{2,1,0:T(8,128)(2,1)S(1)} %bitcast.9) | data formatting | bytes 32768
  37.9 1.8 %copy.11 = bf16[1,256,768]{2,1,0:T(8,128)(2,1)} copy(bf16[1,256,768]{2,1,0:T(8,128)(2,1)} %bitcast.7) | data formatting | bytes 786432
Async XLA Ops:
  35.6 1.6 %copy-start = (bf16[256,32]{1,0:T(8,128)(2,1)S(1)}, bf16[256,32]{1,0:T(8,128)(2,1)}, u32[]{:S(2)}) copy-start(bf16[256,32]{1,0:T(8,128)(2,1)} %get-tuple-element.8) | copy-start | bytes 49156

commit v2 on v1

v2 whole, which is shorter than its diff:
```python
import functools

import jax
import jax.numpy as jnp
from jax import lax
from jax.experimental import pallas as pl
from jax.experimental.pallas import tpu as pltpu
from jax.sharding import PartitionSpec as P

R = 32
BIG = 1.0e9
NT = (((1,), (1,)), ((), ()))


def oddeven_pairs(count):
    pairs = []

    def merge(lo, hi, r):
        step = r * 2
        if step < hi - lo:
            merge(lo, hi, step)
            merge(lo + r, hi, step)
            pairs.extend((i, i + r) for i in range(lo + r, hi - r, step))
        else:
            pairs.append((lo, lo + r))

    def sort(lo, hi):
        if hi - lo >= 1:
            mid = lo + (hi - lo) // 2
            sort(lo, mid)
            sort(mid + 1, hi)
            merge(lo, hi, 1)

    sort(0, count - 1)
    return pairs


PAIRS = oddeven_pairs(R)


def exchange(items, i, j):
    a, b = items[i], items[j]
    items[i], items[j] = jnp.minimum(a, b), jnp.maximum(a, b)


def sort_list(items):
    items = list(items)
    for i, j in PAIRS:
        exchange(items, i, j)
    return items


def merge_low(first, second):
    items = [jnp.minimum(first[i], second[R - 1 - i]) for i in range(R)]
    half = R // 2
    while half:
        for i in range(R):
            if not i & half:
                exchange(items, i, i + half)
        half //= 2
    return items


def dot(a, b):
    return jnp.dot(a, b, preferred_element_type=jnp.float32)


def dot_nt(a, b):
    return lax.dot_general(a, b, NT, preferred_element_type=jnp.float32)


def iota(shape, dim):
    return lax.broadcasted_iota(jnp.int32, shape, dim)


def onehot(cond):
    return jnp.where(cond, 1.0, 0.0).astype(jnp.bfloat16)


def kernel(n, doms, cap, *refs):
    refs = list(refs)
    vec, shards_hbm, locs_hbm, part_hbm = refs[:4]
    refs = refs[4:]
    wide = shards_hbm.shape[0] > 1
    slot_shard_hbm = refs.pop(0) if wide else None
    out_vec, out_rows = refs[:2]
    (own_ref, shards_t, locs, part, slot_shard, sbuf, sinfo, rvec, rinfo, dvec, dpart, posn, ltile, lshard, selfid,
     onorm, dist, lists, rows, srows, drows,
     in_sem, vs_sem, vr_sem, is_sem, ir_sem, ds_sem, dr_sem, ps_sem, pr_sem, rs_sem, rr_sem) = refs[2:]
    per, depth = vec.shape
    list_len = locs.shape[0]
    groups = cap // 8
    lanes = groups * list_len
    me = lax.axis_index("pts")
    dom = lax.axis_index("dom")
    bar = pltpu.get_barrier_semaphore()
    fetches = [pltpu.make_async_copy(shards_hbm, shards_t, in_sem.at[0]),
               pltpu.make_async_copy(locs_hbm, locs, in_sem.at[1]),
               pltpu.make_async_copy(part_hbm, part, in_sem.at[2]),
               pltpu.make_async_copy(vec, own_ref, in_sem.at[3])]
    if wide:
        fetches.append(pltpu.make_async_copy(slot_shard_hbm, slot_shard, in_sem.at[4]))
    for fetch in fetches:
        fetch.start()

    def greet_pts(o, carry):
        pl.semaphore_signal(bar, inc=1, device_id={"pts": lax.rem(me + o, n)}, device_id_type=pl.DeviceIdType.MESH)
        return carry

    def greet_dom(o, carry):
        pl.semaphore_signal(bar, inc=1, device_id={"dom": lax.rem(dom + o, doms)}, device_id_type=pl.DeviceIdType.MESH)
        return carry

    lax.fori_loop(1, n, greet_pts, 0)
    lax.fori_loop(1, doms, greet_dom, 0)

    half = n // 2
    side = me // half
    local = lax.rem(me, half)

    def target(o):
        return lax.rem(side + 1 + o // half, 2) * half + lax.rem(local + o, half)

    def source(o):
        return lax.rem(side + 1 + o // half, 2) * half + lax.rem(local + half - lax.rem(o, half), half)

    order = [o for o in range(half + 1, n)] + [o for o in range(half)]

    for fetch in fetches:
        fetch.wait()
    own = own_ref[...]
    upper = onehot(iota((per, per), 0) < iota((per, per), 1))
    targets = iota((n, per), 0)
    member = shards_t[0:1, :] == targets
    for w in range(1, shards_t.shape[0]):
        member = member | (shards_t[w : w + 1, :] == targets)
    rank = dot(onehot(member), upper)
    posn[...] = jnp.where(member, rank, -1.0)
    tile = onehot(lax.rem(iota((list_len, lanes), 1), list_len) == iota((list_len, lanes), 0))

    def spread(ref):
        return lax.dot_general(ref[...].astype(jnp.float32).astype(jnp.bfloat16), tile, (((0,), (0,)), ((), ())),
                               preferred_element_type=jnp.float32)

    ltile[...] = (spread(locs) + 1.0).astype(jnp.bfloat16)
    if wide:
        lshard[...] = spread(slot_shard)
    lane_group = iota((8, lanes), 1) // list_len
    slot_row = iota((cap, per), 0).astype(jnp.float32)

    def fold(full):
        flat = jnp.zeros((8, lanes), jnp.float32)
        for g in range(groups):
            flat = jnp.where(lane_group == g, full[8 * g : 8 * g + 8], flat)
        return flat.astype(jnp.bfloat16)

    batch = 4

    def pack(b, carry):
        dests = [target(b * batch + t) for t in range(batch)]
        picks = [onehot(posn[pl.ds(c, 1), :] == slot_row) for c in dests]
        pick = jnp.concatenate(picks, axis=0)
        packed = dot(pick, own_ref[...]).astype(jnp.bfloat16)
        if not wide:
            full = dot(pick, ltile[...])
        for t, c in enumerate(dests):
            sbuf[c] = packed[t * cap : t * cap + cap]
            if wide:
                entry = jnp.where(lshard[...] == c.astype(jnp.float32), ltile[...].astype(jnp.float32), 0.0)
                sinfo[c] = fold(dot(picks[t], entry.astype(jnp.bfloat16)))
            else:
                sinfo[c] = fold(full[t * cap : t * cap + cap])
        return carry

    if n <= 16:
        for b in range(n // batch):
            pack(b, 0)
    else:
        lax.fori_loop(0, n // batch, pack, 0)

    pl.semaphore_wait(bar, n - 1 + doms - 1)

    def vec_copy(c, slot_s, slot_r):
        return pltpu.make_async_remote_copy(
            src_ref=sbuf.at[c], dst_ref=rvec.at[slot_r], send_sem=vs_sem.at[slot_s], recv_sem=vr_sem.at[slot_r],
            device_id={"pts": c}, device_id_type=pl.DeviceIdType.MESH)

    def info_copy(c, slot_s, slot_r):
        return pltpu.make_async_remote_copy(
            src_ref=sinfo.at[c], dst_ref=rinfo.at[slot_r], send_sem=is_sem.at[slot_s], recv_sem=ir_sem.at[slot_r],
            device_id={"pts": c}, device_id_type=pl.DeviceIdType.MESH)

    def dom_copy(c, slot_r, src, dst, send, recv):
        return pltpu.make_async_remote_copy(
            src_ref=src, dst_ref=dst.at[slot_r], send_sem=send.at[c], recv_sem=recv.at[slot_r],
            device_id={"dom": c}, device_id_type=pl.DeviceIdType.MESH)

    def send_dom(o, carry):
        c = lax.rem(dom + o, doms)
        dom_copy(c, dom, part, dpart, ps_sem, pr_sem).start()
        dom_copy(c, dom, own_ref, dvec, ds_sem, dr_sem).start()
        return carry

    for o in order:
        c = target(o)
        info_copy(c, c, me).start()
        vec_copy(c, c, me).start()
    lax.fori_loop(1, doms, send_dom, 0)

    square = jnp.square(own.astype(jnp.float32))
    high = square.astype(jnp.bfloat16)
    low = (square - high.astype(jnp.float32)).astype(jnp.bfloat16)
    ones = jnp.ones((8, depth), jnp.bfloat16)
    onorm[...] = dot_nt(ones, high) + dot_nt(ones, low)
    id_tile = (iota((per, 128), 0) + 1).astype(jnp.float32).astype(jnp.bfloat16)
    selfid[...] = dot(onehot(posn[pl.ds(me, 1), :] == slot_row), id_tile)
    rvec[me] = sbuf[me]
    rinfo[me] = sinfo[me]
    dvec[dom] = own
    dpart[dom] = part[...]
    point = (iota((8, per), 1) + 1).astype(jnp.float32)
    width = shards_t.shape[0]

    def join(s, same):
        cand = rvec[s]
        wide_cand = cand.astype(jnp.float32)
        norm = jnp.sum(wide_cand * wide_cand, axis=1, keepdims=True)
        value = (onorm[0:1, :] + norm - 2.0 * dot_nt(cand, own_ref[...])) * (1.0 / depth)
        entry = rinfo[s].astype(jnp.float32)
        reverse, joined = [], []
        for g in range(groups):
            at = g * list_len
            listed = entry[:, at : at + 1] == point
            for k in range(1, list_len):
                listed = listed | (entry[:, at + k : at + k + 1] == point)
            allowed = entry[:, at : at + 1] > 0.0
            for w in range(1, width):
                allowed = allowed | (entry[:, at + w : at + w + 1] > 0.0)
            if same:
                allowed = allowed & (selfid[8 * g : 8 * g + 8, 0:1] != point)
            block = jnp.where(allowed, value[8 * g : 8 * g + 8], BIG)
            joined.append(block)
            reverse.append(jnp.where(listed, block, BIG))
        dist[0, s] = jnp.concatenate(reverse, axis=0).astype(jnp.bfloat16)
        dist[1, s] = jnp.concatenate(joined, axis=0).astype(jnp.bfloat16)

    join(me, True)

    def take(o, carry):
        s = source(lax.rem(o + half, n))
        info_copy(s, s, s).wait_recv()
        vec_copy(s, s, s).wait_recv()
        join(s, False)
        return carry

    def take_dom(o, carry):
        s = lax.rem(dom + doms - o, doms)
        dom_copy(s, s, part, dpart, ps_sem, pr_sem).wait_recv()
        dom_copy(s, s, own_ref, dvec, ds_sem, dr_sem).wait_recv()
        return carry

    def selections():
        base = jnp.zeros((8, 1), jnp.float32)
        for d in range(doms):
            here = jnp.broadcast_to(dpart[d], (8, per)) == dom
            flag = jnp.where(here, 1.0, 0.0)
            place = jnp.where(here, dot(flag.astype(jnp.bfloat16), upper) + base, -1.0)
            base = base + jnp.sum(flag, axis=1, keepdims=True)
            yield d, onehot(place[0:1, :] == iota((per, per), 0).astype(jnp.float32))

    lax.fori_loop(1, half, take, 0)
    lax.fori_loop(1, doms, take_dom, 0)
    total = jnp.zeros((per, depth), jnp.float32)
    for d, pick in selections():
        total = total + dot(pick, dvec[d])
    out_vec[...] = total.astype(jnp.bfloat16)
    lax.fori_loop(half, n, take, 0)

    blocks = cap // 16
    sources = R // blocks
    chunks = n // sources
    tiles = per // 128

    def sort_one(which, tile_id):
        columns = slice(tile_id * 128, tile_id * 128 + 128)

        def chunk(t):
            items = []
            for a in range(sources):
                for b in range(blocks):
                    items.append(dist[which, t * sources + a, 16 * b : 16 * b + 16, columns])
            items = [x.astype(jnp.float32) for x in sort_list(items)]
            return merge_low([x[:8] for x in items], [x[8:] for x in items])

        if chunks == 1:
            items = chunk(0)
            for i in range(R):
                lists[tile_id, i] = items[i]
        else:
            for i in range(R):
                lists[tile_id, i] = jnp.full((8, 128), BIG, jnp.float32)

            def more(t, carry):
                items = merge_low([lists[tile_id, i] for i in range(R)], chunk(t))
                for i in range(R):
                    lists[tile_id, i] = items[i]
                return carry

            lax.fori_loop(0, chunks, more, 0)

    upper_half = iota((8, 128), 0) < 4

    def both(which, carry):
        for tile_id in range(tiles):
            sort_one(which, tile_id)
        for pair in range(tiles // 2):
            first, second = [], []
            for i in range(R):
                a, b = lists[2 * pair, i], lists[2 * pair + 1, i]
                first.append(jnp.where(upper_half, a, b))
                second.append(pltpu.roll(jnp.where(upper_half, b, a), 4, 0))
            items = merge_low(first, second)
            for shift in (6, 7):
                items = merge_low(items, [pltpu.roll(x, shift, 0) for x in items])
            for i in range(R):
                x = jnp.where(items[i] < 0.5 * BIG, items[i], 0.0)
                rows[which, i : i + 1, 256 * pair : 256 * pair + 128] = x[0:1]
                rows[which, i : i + 1, 256 * pair + 128 : 256 * pair + 256] = x[4:5]
        srows[which] = rows[which].astype(jnp.bfloat16)
        return carry

    def rows_copy(c, slot_r, which):
        return pltpu.make_async_remote_copy(
            src_ref=srows.at[which], dst_ref=drows.at[slot_r, which], send_sem=rs_sem.at[which, c],
            recv_sem=rr_sem.at[which, slot_r], device_id={"dom": c}, device_id_type=pl.DeviceIdType.MESH)

    for which in range(2):
        both(which, 0)

        def send_rows(o, carry):
            rows_copy(lax.rem(dom + o, doms), dom, which).start()
            return carry

        lax.fori_loop(1, doms, send_rows, 0)
    drows[dom] = srows[...]

    def take_rows(o, carry):
        s = lax.rem(dom + doms - o, doms)
        rows_copy(s, s, 0).wait_recv()
        rows_copy(s, s, 1).wait_recv()
        return carry

    lax.fori_loop(1, doms, take_rows, 0)
    moved = jnp.zeros((2 * R, per), jnp.float32)
    for d, pick in selections():
        moved = moved + dot_nt(jnp.concatenate([drows[d, 0], drows[d, 1]], axis=0), pick)
    out_rows[...] = moved.astype(jnp.bfloat16)

    def drain_pts(o, carry):
        c = lax.rem(me + o, n)
        info_copy(c, c, me).wait_send()
        vec_copy(c, c, me).wait_send()
        return carry

    def drain_dom(o, carry):
        c = lax.rem(dom + o, doms)
        dom_copy(c, dom, part, dpart, ps_sem, pr_sem).wait_send()
        dom_copy(c, dom, own_ref, dvec, ds_sem, dr_sem).wait_send()
        rows_copy(c, dom, 0).wait_send()
        rows_copy(c, dom, 1).wait_send()
        return carry

    lax.fori_loop(1, n, drain_pts, 0)
    lax.fori_loop(1, doms, drain_dom, 0)


def place(found_vec, found_rows, out_vec, out_rev, out_join):
    out_vec[...] = found_vec[...]
    out_rev[...] = found_rows[:R]
    out_join[...] = found_rows[R:]


def solution(mesh):
    n, doms = mesh.shape["pts"], mesh.shape["dom"]

    def per_device(vectors, neighbor_shards, neighbor_locals, partition):
        per, depth = vectors.shape[1:]
        width = neighbor_shards.shape[2]
        list_len = neighbor_locals.shape[2]
        cap = per // 8
        lanes = (cap // 8) * list_len
        operands = [vectors[0], neighbor_shards[0].T, neighbor_locals[0].T, partition]
        if width > 1:
            operands.append(neighbor_shards[0].T[jnp.arange(list_len) % width])
        bf16, f32, i32 = jnp.bfloat16, jnp.float32, jnp.int32
        dma = pltpu.SemaphoreType.DMA
        vmem = pl.BlockSpec(memory_space=pltpu.VMEM)
        anywhere = pl.BlockSpec(memory_space=pltpu.HBM)
        shapes = (jax.ShapeDtypeStruct((per, depth), bf16), jax.ShapeDtypeStruct((2 * R, per), bf16))
        found_vec, found_rows = pl.pallas_call(
            functools.partial(kernel, n, doms, cap),
            out_shape=shapes,
            in_specs=[anywhere] * len(operands),
            out_specs=(vmem, vmem),
            scratch_shapes=[
                pltpu.VMEM((per, depth), bf16),
                pltpu.VMEM((width, per), i32),
                pltpu.VMEM((list_len, per), i32),
                pltpu.VMEM((1, per), i32),
                pltpu.VMEM((list_len, per), i32),
                pltpu.VMEM((n, cap, depth), bf16),
                pltpu.VMEM((n, 8, lanes), bf16),
                pltpu.VMEM((n, cap, depth), bf16),
                pltpu.VMEM((n, 8, lanes), bf16),
                pltpu.VMEM((doms, per, depth), bf16),
                pltpu.VMEM((doms, 1, per), i32),
                pltpu.VMEM((n, per), f32),
                pltpu.VMEM((per, lanes), bf16),
                pltpu.VMEM((per, lanes), f32),
                pltpu.VMEM((cap, 128), f32),
                pltpu.VMEM((8, per), f32),
                pltpu.VMEM((2, n, cap, per), bf16),
                pltpu.VMEM((per // 128, R, 8, 128), f32),
                pltpu.VMEM((2, R, per), f32),
                pltpu.VMEM((2, R, per), bf16),
                pltpu.VMEM((doms, 2, R, per), bf16),
                dma((5,)),
                dma((n,)), dma((n,)), dma((n,)), dma((n,)),
                dma((doms,)), dma((doms,)), dma((doms,)), dma((doms,)), dma((2, doms)), dma((2, doms)),
            ],
            compiler_params=pltpu.CompilerParams(
                collective_id=0, has_side_effects=True, vmem_limit_bytes=32 * 1024 * 1024),
        )(*[pltpu.with_memory_space_constraint(x, pltpu.HBM) for x in operands])
        out_vec, out_rev, out_join = pl.pallas_call(
            place,
            out_shape=(shapes[0], jax.ShapeDtypeStruct((R, per), bf16), jax.ShapeDtypeStruct((R, per), bf16)),
            in_specs=[vmem, vmem],
            out_specs=(vmem, vmem, vmem),
            compiler_params=pltpu.CompilerParams(vmem_limit_bytes=8 * 1024 * 1024),
        )(found_vec, found_rows)
        return out_vec[None], out_rev.T[None], out_join.T[None]

    return jax.shard_map(
        per_device,
        mesh=mesh,
        in_specs=(
            P("dom", "pts", None),
            P("dom", "pts", None),
            P("dom", "pts", None),
            P("dom", "pts"),
        ),
        out_specs=(P("dom", "pts", None), P("dom", "pts", None), P("dom", "pts", None)),
        check_vma=False,
    )
```

time: 39.9 us -> 32.5 us (0.81)
  the two profiles are of different devices: /device:TPU:25 before, /device:TPU:0 now
where the time goes in v2:
time: 32.5 us; the launch traced here: 32.4 us
  Pallas kernels  31.7 us (98%)
  between operations  0.64 us (2%)
    pallas_call x1, Pallas kernels, per_device(): pl.pallas_call(functools.partial(kernel, n, doms, cap), out_shape=shapes,...  31 us
    pallas_call x1, Pallas kernels, per_device(): pl.pallas_call(place, out_shape=(shapes[0], jax.ShapeDtypeStruct((R, per)...  0.78 us

profile of v2, /device:TPU:0, one launch (start us, length us, event | category | flops | bytes accessed | tf_op | source)
XLA Modules:
  0.0 32.4 jit_solution(15435595964712219124)
XLA Ops:
  0.6 31.0 %shard_map.67 = (bf16[256,768]{1,0:T(8,128)(2,1)S(1)}, bf16[64,256]{1,0:T(8,128)(2,1)S(1)}) custom-call(bf16[256,768]{1,0:T(8,128)(2,1)} %bitcast.12, s32[1,256]{1,0:T(1,128)} %bitcast.14, s32[32,256]{1,0:T(8,128)} %bitcast.13, s32[1,256]{1,0:T(1,128)} %refs_3_.1), custom_call_target="tpu_custom_call" | custom-call | tf_op jit(solution)/shard_map/pallas_call | solution.py:400
  31.6 0.8 %shard_map.68 = (bf16[256,768]{1,0:T(8,128)(2,1)}, bf16[32,256]{1,0:T(8,128)(2,1)}, bf16[32,256]{1,0:T(8,128)(2,1)}) custom-call(bf16[256,768]{1,0:T(8,128)(2,1)S(1)} %get-tuple-element.8.found_vec, bf16[64,256]{1,0:T(8,128)(2,1)S(1)} %get-tuple-element.9.found_rows), custom_call_target="tpu_custom_call" | custom-call | tf_op jit(solution)/shard_map/pallas_call | solution.py:434

commit v3 on v2

--- a/solution.py
+++ b/solution.py
@@ -124,7 +124,7 @@
     def source(o):
         return lax.rem(side + 1 + o // half, 2) * half + lax.rem(local + half - lax.rem(o, half), half)
 
-    order = [o for o in range(half + 1, n)] + [o for o in range(half)]
+    order = [o for o in range(half + 1, n)] + [o * 3 % half for o in range(half)]
 
     for fetch in fetches:
         fetch.wait()
@@ -246,8 +246,8 @@
 
     join(me, True)
 
-    def take(o, carry):
-        s = source(lax.rem(o + half, n))
+    def take(o, carry, near=False):
+        s = source(lax.rem(o + half, n) if near else lax.rem((o - half) * 3, half))
         info_copy(s, s, s).wait_recv()
         vec_copy(s, s, s).wait_recv()
         join(s, False)
@@ -268,7 +268,7 @@
             base = base + jnp.sum(flag, axis=1, keepdims=True)
             yield d, onehot(place[0:1, :] == iota((per, per), 0).astype(jnp.float32))
 
-    lax.fori_loop(1, half, take, 0)
+    lax.fori_loop(1, half, functools.partial(take, near=True), 0)
     lax.fori_loop(1, doms, take_dom, 0)
     total = jnp.zeros((per, depth), jnp.float32)
     for d, pick in selections():

time: 32.5 us -> 32.2 us (level)
    pallas_call x1, Pallas kernels: 31 us -> 30.6 us  [per_device(): pl.pallas_call(functools.partial(kernel, n, doms, cap), out_shape=shapes,...]
where the time goes in v3:
time: 32.2 us; the launch traced here: 32 us
  Pallas kernels  31.4 us (98%)
  between operations  0.64 us (2%)
    pallas_call x1, Pallas kernels, per_device(): pl.pallas_call(functools.partial(kernel, n, doms, cap), out_shape=shapes,...  30.6 us
    pallas_call x1, Pallas kernels, per_device(): pl.pallas_call(place, out_shape=(shapes[0], jax.ShapeDtypeStruct((R, per)...  0.78 us

profile of v3, /device:TPU:0, one launch (start us, length us, event | category | flops | bytes accessed | tf_op | source)
XLA Modules:
  0.0 32.0 jit_solution(9988914235751100648)
XLA Ops:
  0.6 30.6 %shard_map.67 = (bf16[256,768]{1,0:T(8,128)(2,1)S(1)}, bf16[64,256]{1,0:T(8,128)(2,1)S(1)}) custom-call(bf16[256,768]{1,0:T(8,128)(2,1)} %bitcast.12, s32[1,256]{1,0:T(1,128)} %bitcast.14, s32[32,256]{1,0:T(8,128)} %bitcast.13, s32[1,256]{1,0:T(1,128)} %refs_3_.1), custom_call_target="tpu_custom_call" | custom-call | tf_op jit(solution)/shard_map/pallas_call | solution.py:400
  31.2 0.8 %shard_map.68 = (bf16[256,768]{1,0:T(8,128)(2,1)}, bf16[32,256]{1,0:T(8,128)(2,1)}, bf16[32,256]{1,0:T(8,128)(2,1)}) custom-call(bf16[256,768]{1,0:T(8,128)(2,1)S(1)} %get-tuple-element.8.found_vec, bf16[64,256]{1,0:T(8,128)(2,1)S(1)} %get-tuple-element.9.found_rows), custom_call_target="tpu_custom_call" | custom-call | tf_op jit(solution)/shard_map/pallas_call | solution.py:434
